TPU v7x, 512 devices: a whole 4x4x16 slice. The times are simulated.
512 devices in a mesh: row: 32 (over y_hi, z), col: 16 (over x, y_lo, core).
Axes of the slice: x: 4, y: 4 (y_hi: 2, y_lo: 2; y = y_hi * 2 + y_lo), z: 16, core: 2. Of those that a mesh axis runs over, the one named last changes fastest.
Arguments:
- incoming_evolution_embedding: bfloat16 [64, 512, 64], P(None, 'row'), may hold values from -6 to 6
- learned_affine_stretch: float32 [64], replicated, may hold values from 0.5 to 1.5
- learned_affine_offset: float32 [64], replicated, may hold values from -3 to 3
- lefthand_mapping_tensor: bfloat16 [64, 32], replicated, may hold values from -0.75 to 0.75
- righthand_mapping_tensor: bfloat16 [64, 32], replicated, may hold values from -0.75 to 0.75
- final_outer_matrix: bfloat16 [1024, 128], replicated, may hold values from -0.1875 to 0.1875
- residue_couple_cotangent: bfloat16 [512, 512, 128], P('row', 'col'), may hold values from -6 to 6
Outputs:
- alignment_gradient: bfloat16 [64, 512, 64], P('col', 'row')
- left_weight_gradient: float32 [64, 32], replicated
- right_weight_gradient: float32 [64, 32], replicated
- output_weight_gradient: float32 [1024, 128], replicated
All inputs are finite; a program needn't handle non-finite values.
Results may differ from a plain program's by a relative error of at most 0.0064.
Values may be sent and summed in bfloat16 or wider, within the bound.
No kernel may reach another device: no remote copies, remote signals or barrier semaphores. Data moves between devices by JAX's collectives and lax.ppermute only.
A program may use at most 64 MiB of HBM per device.

v0:
```python
import math

import jax
import jax.numpy as jnp
from jax import lax
from jax.sharding import PartitionSpec as P

highest = lax.Precision.HIGHEST


def broadcast(x, axis, root):
    mine = lax.axis_index(axis) == root
    return lax.psum(jnp.where(mine, x, jnp.zeros_like(x)), axis)


def standardize_features(values, learned_affine_stretch, learned_affine_offset):
    values = values.astype(jnp.float32)
    mean_value = jnp.mean(values, -1, keepdims=True)
    centred = values - mean_value
    variance = jnp.mean(centred * centred, -1, keepdims=True)
    reciprocal_spread_std = lax.rsqrt(variance + 1e-05)
    multiplied_activations = centred * reciprocal_spread_std
    standardized_activations = (
        multiplied_activations * learned_affine_stretch + learned_affine_offset
    ).astype(jnp.bfloat16)
    return (multiplied_activations, reciprocal_spread_std, standardized_activations)


def project(standardized_activations, weight):
    array_shape = standardized_activations.shape
    flat = jnp.dot(
        standardized_activations.reshape(-1, array_shape[-1]),
        weight,
        preferred_element_type=jnp.float32,
    )
    return flat.astype(jnp.bfloat16).reshape(array_shape[:-1] + (weight.shape[1],))


def outer_block(left_block, right_matrix, grad_block, final_outer_matrix, element_number, hidden):
    rows = grad_block.shape[0]
    cols = grad_block.shape[1]
    outer = lax.dot_general(
        left_block, right_matrix, (((0,), (0,)), ((), ())), preferred_element_type=jnp.float32
    )
    outer = (outer * (1.0 / element_number)).astype(jnp.bfloat16)
    outer = (
        outer.reshape(rows, hidden, cols, hidden)
        .transpose(0, 2, 1, 3)
        .reshape(rows * cols, hidden * hidden)
    )
    flat_grad = grad_block.reshape(rows * cols, grad_block.shape[2])
    weight_term = lax.dot_general(
        outer, flat_grad, (((0,), (0,)), ((), ())), preferred_element_type=jnp.float32
    )
    outer_grad = lax.dot_general(
        flat_grad, final_outer_matrix, (((1,), (1,)), ((), ())), preferred_element_type=jnp.float32
    )
    outer_grad = outer_grad.astype(jnp.bfloat16)
    outer_grad = (
        outer_grad.reshape(rows, cols, hidden, hidden)
        .transpose(0, 2, 1, 3)
        .reshape(rows * hidden, cols * hidden)
    )
    left_term = lax.dot_general(
        outer_grad, right_matrix, (((1,), (1,)), ((), ())), preferred_element_type=jnp.float32
    )
    left_term = (
        (left_term * (1.0 / element_number))
        .reshape(rows, hidden, element_number)
        .transpose(2, 0, 1)
    )
    right_term = jnp.dot(left_block, outer_grad, preferred_element_type=jnp.float32) * (
        1.0 / element_number
    )
    return (weight_term, left_term, right_term)


def norm_gradient_pass(
    left_gradient,
    right_gradient,
    lefthand_mapping_tensor,
    righthand_mapping_tensor,
    multiplied_activations,
    reciprocal_spread_std,
    learned_affine_stretch,
):
    hidden = lefthand_mapping_tensor.shape[1]
    hidden_grad = jnp.dot(
        left_gradient.reshape(-1, hidden),
        lefthand_mapping_tensor.astype(jnp.float32).T,
        precision=highest,
    )
    hidden_grad = hidden_grad + jnp.dot(
        right_gradient.reshape(-1, hidden),
        righthand_mapping_tensor.astype(jnp.float32).T,
        precision=highest,
    )
    hidden_grad = hidden_grad.reshape(multiplied_activations.shape) * learned_affine_stretch
    mean_one = jnp.mean(hidden_grad, -1, keepdims=True)
    mean_two = jnp.mean(hidden_grad * multiplied_activations, -1, keepdims=True)
    return (
        reciprocal_spread_std * (hidden_grad - mean_one - multiplied_activations * mean_two)
    ).astype(jnp.bfloat16)


def weight_grad(standardized_activations, factor_grad):
    feature_width = standardized_activations.shape[-1]
    hidden = factor_grad.shape[-1]
    return lax.dot_general(
        standardized_activations.astype(jnp.float32).reshape(-1, feature_width),
        factor_grad.reshape(-1, hidden),
        (((0,), (0,)), ((), ())),
        precision=highest,
        preferred_element_type=jnp.float32,
    )


def on_device(
    incoming_evolution_embedding,
    learned_affine_stretch,
    learned_affine_offset,
    lefthand_mapping_tensor,
    righthand_mapping_tensor,
    final_outer_matrix,
    residue_couple_cotangent,
):
    homolog_number, residue_slices, feature_width = incoming_evolution_embedding.shape
    hidden = lefthand_mapping_tensor.shape[1]
    cohort_extent = lax.axis_size("row") // lax.axis_size("col")
    residue_position = lax.axis_index("col")
    row_index = lax.axis_index("row")
    multiplied_activations, reciprocal_spread_std, standardized_activations = standardize_features(
        incoming_evolution_embedding, learned_affine_stretch, learned_affine_offset
    )
    left_factor = project(standardized_activations, lefthand_mapping_tensor)
    divide_pieces = []
    for cohort_rank in range(cohort_extent):
        divide_pieces.append(
            broadcast(
                incoming_evolution_embedding, "row", cohort_extent * residue_position + cohort_rank
            )
        )
    fetched = jnp.concatenate(divide_pieces, 1)
    fetched_normed = standardize_features(fetched, learned_affine_stretch, learned_affine_offset)[2]
    right_cols = project(fetched_normed, righthand_mapping_tensor)
    tok_cols = right_cols.shape[1]
    right_matrix = right_cols.reshape(homolog_number, tok_cols * hidden)
    block_rows = math.gcd(residue_slices, 8)
    weight_acc = jnp.zeros((hidden * hidden, final_outer_matrix.shape[1]), jnp.float32)
    right_acc = jnp.zeros((homolog_number, tok_cols * hidden), jnp.float32)
    left_parts = []
    for offset in range(0, residue_slices, block_rows):
        left_block = left_factor[:, offset : offset + block_rows, :].reshape(
            homolog_number, block_rows * hidden
        )
        grad_block = residue_couple_cotangent[offset : offset + block_rows]
        weight_term, left_term, right_term = outer_block(
            left_block, right_matrix, grad_block, final_outer_matrix, homolog_number, hidden
        )
        weight_acc = weight_acc + weight_term
        right_acc = right_acc + right_term
        left_parts.append(left_term)
    left_partial = jnp.concatenate(left_parts, 1)
    left_gradient = lax.psum_scatter(left_partial, "col", scatter_dimension=0, tiled=True)
    seq_share = homolog_number // lax.axis_size("col")
    seq_first = residue_position * seq_share
    right_partial = right_acc.reshape(homolog_number, tok_cols, hidden)
    right_total = lax.psum(right_partial, "row")
    own_part = lax.dynamic_slice_in_dim(
        right_total, row_index % cohort_extent * residue_slices, residue_slices, 1
    )
    right_rows = broadcast(own_part, "col", row_index // cohort_extent)
    right_gradient = lax.dynamic_slice_in_dim(right_rows, seq_first, seq_share, 0)
    scaled_own_part = lax.dynamic_slice_in_dim(multiplied_activations, seq_first, seq_share, 0)
    inverse_own_scale = lax.dynamic_slice_in_dim(reciprocal_spread_std, seq_first, seq_share, 0)
    normed_own = lax.dynamic_slice_in_dim(standardized_activations, seq_first, seq_share, 0)
    alignment_gradient = norm_gradient_pass(
        left_gradient,
        right_gradient,
        lefthand_mapping_tensor,
        righthand_mapping_tensor,
        scaled_own_part,
        inverse_own_scale,
        learned_affine_stretch,
    )
    left_weight = weight_grad(normed_own, left_gradient)
    right_weight = weight_grad(normed_own, right_gradient)
    out_total, left_total, right_sum = lax.psum(
        (weight_acc, left_weight, right_weight), ("row", "col")
    )
    tokens = residue_slices * lax.axis_size("row")
    return (
        alignment_gradient,
        left_total * (1.0 / tokens),
        right_sum * (1.0 / tokens),
        out_total * (1.0 / tokens),
    )


def solution(mesh):
    in_specs = (P(None, "row", None), P(), P(), P(), P(), P(), P("row", "col", None))
    out_specs = (P("col", "row", None), P(), P(), P())
    return jax.shard_map(
        on_device, mesh=mesh, in_specs=in_specs, out_specs=out_specs, check_vma=False
    )
```

profile of v0, /device:TPU:1, one launch (start us, length us, event | category | flops | bytes accessed | tf_op | source)
XLA Modules:
  0.0 1406.3 jit_solution(8164136535824600437)
XLA Ops:
  7.2 1.8 broadcast_select_fusion.1
  12.7 1.6 reshape.145
  14.2 2.1 copy.62
  16.4 3.6 reshape.146
  23.3 1.6 reshape.149
  24.8 2.1 copy.61
  27.0 3.6 reshape.150
  31.1 1.8 copy.51
  33.0 265.5 %all-reduce.13.cloned.1.call-done = (bf16[64,16,64]{2,1,0:T(8,128)(2,1)}, bf16[64,16,64]{2,1,0:T(8,128)(2,1)}) async-done(((bf16[64,16,64]{2,1,0:T(8,128)(2,1)}, bf16[64,16,64]{2,1,0:T(8,128)(2,1)}), (bf16[64,16,64]{2,1,0:T(8,128)(2,1)}, bf16[64,16,64]{2,1,0:T(8,128)(2,1)})) %all-reduce.13.cloned.1.call-update) | async-done | bytes 262160 | tf_op jit(solution)/shard_map/psum | solution.py:13
  299.7 1.4 fusion.10
  305.9 290.3 %all-reduce.7.cloned.1.call-done = f32[64,32,32]{2,1,0:T(8,128)} async-done(((f32[64,32,32]{2,1,0:T(8,128)}), f32[64,32,32]{2,1,0:T(8,128)}) %all-reduce.7.cloned.1.call-update) | async-done | bytes 262160 | tf_op jit(solution)/shard_map/psum | solution.py:168
  596.2 1.9 dynamic-slice_select_fusion
  598.3 2.9 reshape.160
  601.2 2.1 copy.60
  603.3 3.6 reshape.161
  608.0 2.8 reshape.162
  610.9 2.1 copy.59
  613.0 3.6 reshape.163
  619.8 129.4 %all-reduce.9.cloned.1.call-done = f32[64,16,32]{2,1,0:T(8,128)} async-done(((f32[64,16,32]{2,1,0:T(8,128)}), f32[64,16,32]{2,1,0:T(8,128)}) %all-reduce.9.cloned.1.call-update) | async-done | bytes 131088 | tf_op jit(solution)/shard_map/psum | solution.py:13
  750.9 470.0 %all-reduce.11.cloned.1.call-done = f32[1024,128]{1,0:T(8,128)} async-done(((f32[1024,128]{1,0:T(8,128)}), f32[1024,128]{1,0:T(8,128)}) %all-reduce.11.cloned.1.call-update) | async-done | bytes 524304 | tf_op jit(solution)/shard_map/psum | solution.py:188
  1220.9 1.9 broadcast_multiply_fusion
  1222.8 64.8 %reduce-scatter.2.cloned.1.call-done = f32[4,16,32]{2,1,0:T(8,128)} async-done(((f32[64,16,32]{2,1,0:T(8,128)}), f32[4,16,32]{2,1,0:T(8,128)}) %reduce-scatter.2.cloned.1.call-update) | async-done | bytes 8208 | tf_op jit(solution)/shard_map/reduce_scatter | solution.py:164
  1291.5 106.2 %all-reduce = (f32[64,32]{0,1:T(8,128)S(1)}, f32[64,32]{0,1:T(8,128)S(1)}) all-reduce(f32[64,32]{0,1:T(8,128)S(1)} %convolution_bitcast_fusion.1, f32[64,32]{0,1:T(8,128)S(1)} %convolution_bitcast_fusion), channel_id=1, replica_groups=mesh['row'=32,'col'=16] {'row','col'}, use_global_device_ids=true, to_apply=%region_11.12 | all-reduce | flops 4096 | bytes 32768 | tf_op jit(solution)/shard_map/psum | solution.py:188
  1398.3 1.5 multiply_convert_fusion
  (101 shorter events, 24.0 us)
Async XLA Ops:
  7.2 4.6 copy-start
  7.2 4.5 copy-start.14
  7.2 291.3 %all-reduce.13.cloned.1.call-start = ((), (), s32[]{:S(2)}) async-start(), calls=%async_computation.5 | async-start | bytes 1048576 | tf_op jit(solution)/shard_map/psum | solution.py:13
  9.1 587.1 %all-reduce.7.cloned.1.call-start = ((), (), s32[]{:S(2)}) async-start(), calls=%async_computation.2 | async-start | bytes 2097152 | tf_op jit(solution)/shard_map/psum | solution.py:168
  11.7 8.3 copy-start.13
  16.4 3.6 copy-start.1
  16.4 3.6 copy-start.17
  16.4 3.6 copy-start.20
  16.4 4.8 copy-start.15
  21.2 0.7 copy-start.5
  27.0 3.7 copy-start.6
  32.9 269.0 %copy-start.18 = (f32[64]{0:T(128)S(1)}, f32[64]{0:T(128)}, u32[]{:S(2)}) copy-start(f32[64]{0:T(128)} %param.8) | copy-start | bytes 772
  32.9 269.0 %copy-start.21 = (f32[64]{0:T(128)S(1)}, f32[64]{0:T(128)}, u32[]{:S(2)}) copy-start(f32[64]{0:T(128)} %param.9) | copy-start | bytes 772
  33.0 716.2 %all-reduce.9.cloned.1.call-start = ((), (), s32[]{:S(2)}) async-start(), calls=%async_computation.3 | async-start | bytes 1048576 | tf_op jit(solution)/shard_map/psum | solution.py:13
  298.5 2.6 copy-start.2
  298.5 2.6 copy-start.3
  298.5 4.1 copy-start.16
  301.1 2.5 copy-start.12
  598.1 622.8 %all-reduce.11.cloned.1.call-start = ((), (), s32[]{:S(2)}) async-start(), calls=%async_computation.4 | async-start | bytes 1048576 | tf_op jit(solution)/shard_map/psum | solution.py:188
  603.3 3.6 copy-start.10
  613.0 3.6 copy-start.4
  613.0 3.6 copy-start.8
  618.2 670.3 %copy-start.19 = (f32[64]{0:T(128)S(1)}, f32[64]{0:T(128)}, u32[]{:S(2)}) copy-start(f32[64]{0:T(128)} %param.8) | copy-start | bytes 772
  618.3 669.3 %reduce-scatter.2.cloned.1.call-start = ((), (), s32[]{:S(2)}) async-start(), calls=%async_computation.1 | async-start | bytes 557056 | tf_op jit(solution)/shard_map/reduce_scatter | solution.py:164
  (3 other events, 1.9 us)
Sparse Core Ops, SparseCore 0:
  11.5 286.9 all-reduce.12
  301.4 294.7 all-reduce.6
  599.7 149.4 all-reduce.8
  754.5 466.3 all-reduce.10
  1223.5 64.0 reduce-scatter.1
where the time goes:
time: 1410 us
  waiting for transfers between devices  1220 us (87%)
  blocking collectives  106 us (8%)
  local copies, waits for them, and re-layouts  38.3 us (3%)
  other arithmetic  16.7 us (1%)
  between operations  14.3 us (1%)
    psum x1, waiting for transfers between devices, on_device(): lax.psum((weight_acc, left_weight, right_weight), ('row', 'col'))  470 us
    psum x2, waiting for transfers between devices, broadcast(): return lax.psum(jnp.where(mine, x, jnp.zeros_like(x)), axis)  395 us
    psum x1, waiting for transfers between devices, on_device(): right_total = lax.psum(right_partial, 'row')  290 us
    psum x1, blocking collectives, on_device(): lax.psum((weight_acc, left_weight, right_weight), ('row', 'col'))  106 us
    reduce_scatter x1, waiting for transfers between devices, on_device(): lax.psum_scatter(left_partial, 'col', scatter_dimension=0, tiled=True)  64.8 us
  transfers between devices with their start and end apart: 5, of which 5 were waited for; matrix products, arithmetic and copies ran while one was open for 4% of the time, Pallas kernels for 0%

commit v1 on v0

--- a/solution.py
+++ b/solution.py
@@ -8,9 +8,49 @@
 highest = lax.Precision.HIGHEST
 
 
-def broadcast(x, axis, root):
-    mine = lax.axis_index(axis) == root
-    return lax.psum(jnp.where(mine, x, jnp.zeros_like(x)), axis)
+def swap_pairs(rows, cols, turn):
+    ratio = rows // cols
+    return [
+        (
+            source * cols + copy,
+            (ratio * copy + (source + turn) % ratio) * cols + source // ratio,
+        )
+        for source in range(rows)
+        for copy in range(cols)
+    ]
+
+
+def home_pairs(rows, cols):
+    ratio = rows // cols
+    return [
+        ((half * cols + share) * cols + col, (ratio * col + half) * cols + share)
+        for half in range(ratio)
+        for share in range(cols)
+        for col in range(cols)
+    ]
+
+
+def swap_tokens(own, row_index, rows, cols):
+    ratio = rows // cols
+    arrived = [
+        lax.ppermute(own, ("row", "col"), swap_pairs(rows, cols, turn)) for turn in range(ratio)
+    ]
+    ordered = []
+    for part in range(ratio):
+        chosen = arrived[0]
+        for turn in range(1, ratio):
+            chosen = jnp.where((row_index - turn) % ratio == part, arrived[turn], chosen)
+        ordered.append(chosen)
+    return ordered
+
+
+def trade(pieces, axis):
+    return lax.all_to_all(pieces, axis, 0, 0, tiled=True)
+
+
+def spread(piece, axis):
+    extent = lax.axis_size(axis)
+    return trade(jnp.broadcast_to(piece[None], (extent,) + piece.shape), axis)
 
 
 def standardize_features(values, learned_affine_stretch, learned_affine_offset):
@@ -126,27 +166,23 @@
 ):
     homolog_number, residue_slices, feature_width = incoming_evolution_embedding.shape
     hidden = lefthand_mapping_tensor.shape[1]
-    cohort_extent = lax.axis_size("row") // lax.axis_size("col")
+    pair_width = final_outer_matrix.shape[1]
+    rows, cols = lax.axis_size("row"), lax.axis_size("col")
+    ratio = rows // cols
     residue_position = lax.axis_index("col")
     row_index = lax.axis_index("row")
     multiplied_activations, reciprocal_spread_std, standardized_activations = standardize_features(
         incoming_evolution_embedding, learned_affine_stretch, learned_affine_offset
     )
+    right_own = project(standardized_activations, righthand_mapping_tensor)
+    right_parts = swap_tokens(
+        right_own.reshape(homolog_number, residue_slices * hidden), row_index, rows, cols
+    )
+    right_matrix = jnp.concatenate(right_parts, 1)
     left_factor = project(standardized_activations, lefthand_mapping_tensor)
-    divide_pieces = []
-    for cohort_rank in range(cohort_extent):
-        divide_pieces.append(
-            broadcast(
-                incoming_evolution_embedding, "row", cohort_extent * residue_position + cohort_rank
-            )
-        )
-    fetched = jnp.concatenate(divide_pieces, 1)
-    fetched_normed = standardize_features(fetched, learned_affine_stretch, learned_affine_offset)[2]
-    right_cols = project(fetched_normed, righthand_mapping_tensor)
-    tok_cols = right_cols.shape[1]
-    right_matrix = right_cols.reshape(homolog_number, tok_cols * hidden)
+    tok_cols = ratio * residue_slices
     block_rows = math.gcd(residue_slices, 8)
-    weight_acc = jnp.zeros((hidden * hidden, final_outer_matrix.shape[1]), jnp.float32)
+    weight_acc = jnp.zeros((hidden * hidden, pair_width), jnp.float32)
     right_acc = jnp.zeros((homolog_number, tok_cols * hidden), jnp.float32)
     left_parts = []
     for offset in range(0, residue_slices, block_rows):
@@ -161,19 +197,48 @@
         right_acc = right_acc + right_term
         left_parts.append(left_term)
     left_partial = jnp.concatenate(left_parts, 1)
-    left_gradient = lax.psum_scatter(left_partial, "col", scatter_dimension=0, tiled=True)
-    seq_share = homolog_number // lax.axis_size("col")
+
+    seq_share = homolog_number // cols
     seq_first = residue_position * seq_share
-    right_partial = right_acc.reshape(homolog_number, tok_cols, hidden)
-    right_total = lax.psum(right_partial, "row")
-    own_part = lax.dynamic_slice_in_dim(
-        right_total, row_index % cohort_extent * residue_slices, residue_slices, 1
-    )
-    right_rows = broadcast(own_part, "col", row_index // cohort_extent)
-    right_gradient = lax.dynamic_slice_in_dim(right_rows, seq_first, seq_share, 0)
+    chunk = (seq_share * residue_slices * hidden // pair_width, pair_width)
+    right_pieces = (
+        right_acc.astype(jnp.bfloat16)
+        .reshape(cols, seq_share, ratio, residue_slices * hidden)
+        .transpose(2, 0, 1, 3)
+        .reshape((rows,) + chunk)
+    )
+    left_pieces = left_partial.astype(jnp.bfloat16).reshape((cols,) + chunk)
+    weight_pieces = weight_acc.astype(jnp.bfloat16).reshape(cols, -1, pair_width)
+    col_taken = trade(jnp.concatenate([left_pieces, weight_pieces], 1), "col")
+    row_taken = trade(right_pieces, "row")
+    right_sum = jnp.sum(row_taken.astype(jnp.float32), 0)
+    right_sum = lax.ppermute(right_sum, ("row", "col"), home_pairs(rows, cols))
+    col_sum = jnp.sum(col_taken.astype(jnp.float32), 0)
+    own_shape = (seq_share, residue_slices, hidden)
+    left_gradient = col_sum[: chunk[0]].reshape(own_shape)
+    right_gradient = right_sum.reshape(own_shape)
+    weight_share = col_sum[chunk[0] :]
+
     scaled_own_part = lax.dynamic_slice_in_dim(multiplied_activations, seq_first, seq_share, 0)
     inverse_own_scale = lax.dynamic_slice_in_dim(reciprocal_spread_std, seq_first, seq_share, 0)
     normed_own = lax.dynamic_slice_in_dim(standardized_activations, seq_first, seq_share, 0)
+    both_weight = weight_grad(
+        normed_own, jnp.concatenate([left_gradient, right_gradient], -1)
+    ).reshape(rows, -1, pair_width)
+    weight_rows = weight_share.shape[0] // rows
+    row_pieces = jnp.concatenate(
+        [weight_share.reshape(rows, weight_rows, pair_width), both_weight], 1
+    )
+    row_sum = jnp.sum(trade(row_pieces, "row"), 0)
+    gathered = spread(row_sum, "row")
+    weight_full = gathered[:, :weight_rows].reshape(-1, pair_width)
+    both_part = gathered[:, weight_rows:].reshape(-1, pair_width)
+    last = spread(jnp.concatenate([weight_full, both_part], 0).astype(jnp.bfloat16), "col")
+    last = last.astype(jnp.float32)
+    tokens = residue_slices * rows
+    output_weight = last[:, : weight_full.shape[0]].reshape(-1, pair_width) * (1.0 / tokens)
+    both_total = jnp.sum(last[:, weight_full.shape[0] :], 0) * (1.0 / tokens)
+    both_total = both_total.reshape(feature_width, 2 * hidden)
     alignment_gradient = norm_gradient_pass(
         left_gradient,
         right_gradient,
@@ -183,18 +248,7 @@
         inverse_own_scale,
         learned_affine_stretch,
     )
-    left_weight = weight_grad(normed_own, left_gradient)
-    right_weight = weight_grad(normed_own, right_gradient)
-    out_total, left_total, right_sum = lax.psum(
-        (weight_acc, left_weight, right_weight), ("row", "col")
-    )
-    tokens = residue_slices * lax.axis_size("row")
-    return (
-        alignment_gradient,
-        left_total * (1.0 / tokens),
-        right_sum * (1.0 / tokens),
-        out_total * (1.0 / tokens),
-    )
+    return (alignment_gradient, both_total[:, :hidden], both_total[:, hidden:], output_weight)
 
 
 def solution(mesh):

time: 1410 us -> 190 us (0.13)
  waiting for transfers between devices: 1220 us -> 59 us
  blocking collectives: 106 us -> 0 us
  starting transfers between devices: 0.39 us -> 73.1 us
    psum x4 -> x0, waiting for transfers between devices: 1160 us -> none  [the longest x1 470 us: on_device(): lax.psum((weight_acc, left_weight, right_weight), ('row', 'col'))]
    psum x1 -> x0, blocking collectives: 106 us -> none  [on_device(): lax.psum((weight_acc, left_weight, right_weight), ('row', 'col'))]
    reduce_scatter x1 -> x0, waiting for transfers between devices: 64.8 us -> none  [on_device(): lax.psum_scatter(left_partial, 'col', scatter_dimension=0, tiled=True)]
    all_to_all x0 -> x5, starting transfers between devices: none -> 59.1 us  [trade(): return lax.all_to_all(pieces, axis, 0, 0, tiled=True)]
    all_to_all x0 -> x5, waiting for transfers between devices: none -> 57.5 us  [trade(): return lax.all_to_all(pieces, axis, 0, 0, tiled=True)]
  transfers between devices with their start and end apart: 5 -> 8, of which waited for: 5 -> 6; matrix products, arithmetic and copies ran while one was open for 4% -> 13% of each run, Pallas kernels for 0% -> 0%
where the time goes in v1:
time: 190 us; the launch traced here: 189 us
  starting transfers between devices  73.1 us (38%)
  waiting for transfers between devices  59 us (31%)
  local copies, waits for them, and re-layouts  38.4 us (20%)
  other arithmetic  11 us (6%)
  matrix products  6.14 us (3%)
    all_to_all x5, starting transfers between devices, trade(): return lax.all_to_all(pieces, axis, 0, 0, tiled=True)  59.1 us
    all_to_all x5, waiting for transfers between devices, trade(): return lax.all_to_all(pieces, axis, 0, 0, tiled=True)  57.5 us
    ppermute x2, starting transfers between devices, swap_tokens(): lax.ppermute(own, ('row', 'col'), swap_pairs(rows, cols, turn))  9.54 us
    reshape x4, local copies, waits for them, and re-layouts, outer_block(): outer_grad.reshape(rows, cols, hidden, hidden).transpose(0, 2, 1, 3)  8.73 us
    reshape x2, local copies, waits for them, and re-layouts, outer_block(): outer_grad = outer_grad.reshape(rows, cols, hidden, hidden).transpose(0,...  8.45 us
    reshape x4, local copies, waits for them, and re-layouts, outer_block(): outer.reshape(rows, hidden, cols, hidden).transpose(0, 2, 1, 3)  7.48 us
    reshape x2, local copies, waits for them, and re-layouts, outer_block(): outer = outer.reshape(rows, hidden, cols, hidden).transpose(0, 2, 1, 3).r...  7.16 us
    ppermute x1, starting transfers between devices, on_device(): right_sum = lax.ppermute(right_sum, ('row', 'col'), home_pairs(rows, cols))  4.48 us
  transfers between devices with their start and end apart: 8, of which 6 were waited for; matrix products, arithmetic and copies ran while one was open for 13% of the time, Pallas kernels for 0%

profile of v1, /device:TPU:1, one launch (start us, length us, event | category | flops | bytes accessed | tf_op | source)
XLA Modules:
  0.0 188.7 jit_solution(17861979072240224247)
XLA Ops:
  3.2 2.1 %add_convert_fusion = (bf16[64,16,64]{2,1,0:T(8,128)(2,1)S(1)}, f32[64,16,64]{2,1,0:T(8,128)}) fusion(f32[64]{0:T(128)} %param.9, f32[64]{0:T(128)} %param.8, f32[64,16]{1,0:T(8,128)S(1)} %add_rsqrt_fusion, f32[64,16]{1,0:T(8,128)S(1)} %broadcast_multiply_fusion, bf16[64,16,64]{2,1,0:T(8,128)(2,1)} %param.7), kind=kLoop, calls=%fused_computation.30 | loop fusion | flops 393216 | bytes 532992 | tf_op jit(solution)/shard_map/convert_element_type | solution.py:65
  7.3 7.6 %collective-permute-start = (bf16[64,512]{1,0:T(8,128)(2,1)}, bf16[64,512]{1,0:T(8,128)(2,1)}, u32[]{:S(2)}, u32[]{:S(2)}) collective-permute-start(bf16[64,512]{1,0:T(8,128)(2,1)} %reshape_reshape.9), channel_id=1, source_target_pairs={{0,16},{1,48},{2,80},{3,112},{4,144},{5,176},{6,208},{7,240},{8,27... | collective-permute-start | bytes 196616 | tf_op jit(solution)/shard_map/ppermute | solution.py:36
  14.9 1.9 %collective-permute-start.1 = (bf16[64,512]{1,0:T(8,128)(2,1)}, bf16[64,512]{1,0:T(8,128)(2,1)}, u32[]{:S(2)}, u32[]{:S(2)}) collective-permute-start(bf16[64,512]{1,0:T(8,128)(2,1)} %reshape_reshape.9), channel_id=1, source_target_pairs={{0,0},{1,32},{2,64},{3,96},{4,128},{5,160},{6,192},{7,224},{8,256}... | collective-permute-start | bytes 196616 | tf_op jit(solution)/shard_map/ppermute | solution.py:36
  19.0 2.9 %reshape.166 = bf16[8,32,32,32]{3,2,1,0:T(8,128)(2,1)S(1)} reshape(bf16[256,1024]{1,0:T(8,128)(2,1)} %convolution_convert_fusion) | data formatting | bytes 1048576 | tf_op jit(solution)/shard_map/reshape | solution.py:100
  21.8 2.2 %copy.57 = bf16[8,32,32,32]{3,1,2,0:T(8,128)(2,1)} copy(bf16[8,32,32,32]{3,2,1,0:T(8,128)(2,1)S(1)} %reshape.166) | data formatting | bytes 1048576 | tf_op jit(solution)/shard_map/reshape | solution.py:100
  24.0 4.2 %reshape.167 = bf16[256,1024]{1,0:T(8,128)(2,1)} reshape(bf16[8,32,32,32]{3,2,1,0:T(8,128)(2,1)} %bitcast.70) | data formatting | bytes 1048576 | tf_op jit(solution)/shard_map/reshape | solution.py:102
  29.8 2.2 %copy.58 = bf16[8,32,32,32]{3,1,2,0:T(8,128)(2,1)} copy(bf16[8,32,32,32]{3,2,1,0:T(8,128)(2,1)S(1)} %reshape.161) | data formatting | bytes 1048576 | tf_op jit(solution)/shard_map/reshape | solution.py:100
  32.0 4.2 %reshape.162 = bf16[256,1024]{1,0:T(8,128)(2,1)} reshape(bf16[8,32,32,32]{3,2,1,0:T(8,128)(2,1)} %bitcast.71) | data formatting | bytes 1048576 | tf_op jit(solution)/shard_map/reshape | solution.py:102
  37.3 1.6 reshape.171
  38.9 2.2 %copy.56 = bf16[8,32,32,32]{3,1,2,0:T(8,128)(2,1)} copy(bf16[8,32,32,32]{3,2,1,0:T(8,128)(2,1)S(1)} %reshape.171) | data formatting | bytes 1048576 | tf_op jit(solution)/shard_map/reshape | solution.py:87
  41.1 3.5 %reshape.172 = bf16[256,1024]{1,0:T(8,128)(2,1)S(1)} reshape(bf16[8,32,32,32]{3,2,1,0:T(8,128)(2,1)} %bitcast.72) | data formatting | bytes 1048576 | tf_op jit(solution)/shard_map/reshape | solution.py:89
  47.6 2.2 %copy.55 = bf16[8,32,32,32]{3,1,2,0:T(8,128)(2,1)} copy(bf16[8,32,32,32]{3,2,1,0:T(8,128)(2,1)S(1)} %reshape.174) | data formatting | bytes 1048576 | tf_op jit(solution)/shard_map/reshape | solution.py:87
  49.8 3.6 %reshape.175 = bf16[256,1024]{1,0:T(8,128)(2,1)S(1)} reshape(bf16[8,32,32,32]{3,2,1,0:T(8,128)(2,1)} %bitcast.73) | data formatting | bytes 1048576 | tf_op jit(solution)/shard_map/reshape | solution.py:89
  55.9 16.3 %all-to-all-start = ((bf16[16,80,128]{2,1,0:T(8,128)(2,1)}), bf16[16,80,128]{2,1,0:T(8,128)(2,1)S(1)}, u32[]{:S(2)}, u32[]{:S(2)}) async-start(bf16[16,80,128]{2,1,0:T(8,128)(2,1)} %pad_maximum_fusion), calls=%async_computation | async-start | bytes 655360 | tf_op jit(solution)/shard_map/all_to_all | solution.py:48
  73.5 6.7 %all-to-all-done = bf16[16,80,128]{2,1,0:T(8,128)(2,1)S(1)} async-done(((bf16[16,80,128]{2,1,0:T(8,128)(2,1)}), bf16[16,80,128]{2,1,0:T(8,128)(2,1)S(1)}, u32[]{:S(2)}, u32[]{:S(2)}) %all-to-all-start) | async-done | bytes 327712 | tf_op jit(solution)/shard_map/all_to_all | solution.py:48
  80.2 15.6 %all-to-all-start.1 = ((bf16[32,16,128]{2,1,0:T(8,128)(2,1)}), bf16[32,16,128]{2,1,0:T(8,128)(2,1)S(1)}, u32[]{:S(2)}, u32[]{:S(2)}) async-start(bf16[32,16,128]{2,1,0:T(8,128)(2,1)} %reshape.178), calls=%async_computation.1 | async-start | bytes 262144 | tf_op jit(solution)/shard_map/all_to_all | solution.py:48
  95.9 16.5 %all-to-all-done.1 = bf16[32,16,128]{2,1,0:T(8,128)(2,1)S(1)} async-done(((bf16[32,16,128]{2,1,0:T(8,128)(2,1)}), bf16[32,16,128]{2,1,0:T(8,128)(2,1)S(1)}, u32[]{:S(2)}, u32[]{:S(2)}) %all-to-all-start.1) | async-done | bytes 131104 | tf_op jit(solution)/shard_map/all_to_all | solution.py:48
  112.5 4.5 %collective-permute-start.2 = (f32[16,128]{1,0:T(8,128)S(1)}, f32[16,128]{1,0:T(8,128)S(1)}, u32[]{:S(2)}, u32[]{:S(2)}) collective-permute-start(f32[16,128]{1,0:T(8,128)S(1)} %convert_reduce_fusion.2), channel_id=1, source_target_pairs={{0,0},{1,32},{2,64},{3,96},{4,128},{5,160},{6,192},{7,224},{8,256}... | collective-permute-start | bytes 24584 | tf_op jit(solution)/shard_map/ppermute | solution.py:215
  120.1 15.2 %all-to-all-start.2 = ((f32[32,3,128]{2,1,0:T(4,128)}), f32[32,3,128]{2,1,0:T(4,128)S(1)}, u32[]{:S(2)}, u32[]{:S(2)}) async-start(f32[32,3,128]{2,1,0:T(4,128)} %pad_maximum_fusion.3), calls=%async_computation.2 | async-start | bytes 131072 | tf_op jit(solution)/shard_map/all_to_all | solution.py:48
  135.4 14.6 %all-to-all-done.2 = f32[32,3,128]{2,1,0:T(4,128)S(1)} async-done(((f32[32,3,128]{2,1,0:T(4,128)}), f32[32,3,128]{2,1,0:T(4,128)S(1)}, u32[]{:S(2)}, u32[]{:S(2)}) %all-to-all-start.2) | async-done | bytes 49184 | tf_op jit(solution)/shard_map/all_to_all | solution.py:48
  150.7 3.8 %all-to-all-start.3 = ((bf16[32,3,128]{2,1,0:T(4,128)(2,1)}), bf16[32,3,128]{2,1,0:T(4,128)(2,1)S(1)}, u32[]{:S(2)}, u32[]{:S(2)}) async-start(bf16[32,3,128]{2,1,0:T(4,128)(2,1)} %broadcast_in_dim.4), calls=%async_computation.3 | async-start | bytes 65536 | tf_op jit(solution)/shard_map/all_to_all | solution.py:48
  155.4 13.2 %all-to-all-done.3 = bf16[32,3,128]{2,1,0:T(4,128)(2,1)S(1)} async-done(((bf16[32,3,128]{2,1,0:T(4,128)(2,1)}), bf16[32,3,128]{2,1,0:T(4,128)(2,1)S(1)}, u32[]{:S(2)}, u32[]{:S(2)}) %all-to-all-start.3) | async-done | bytes 24608 | tf_op jit(solution)/shard_map/all_to_all | solution.py:48
  169.5 8.2 %all-to-all-start.4 = ((bf16[16,96,128]{2,1,0:T(8,128)(2,1)}), bf16[16,96,128]{2,1,0:T(8,128)(2,1)S(1)}, u32[]{:S(2)}, u32[]{:S(2)}) async-start(bf16[16,96,128]{2,1,0:T(8,128)(2,1)} %broadcast_in_dim.5), calls=%async_computation.4 | async-start | bytes 786432 | tf_op jit(solution)/shard_map/all_to_all | solution.py:48
  179.8 6.5 %all-to-all-done.4 = bf16[16,96,128]{2,1,0:T(8,128)(2,1)S(1)} async-done(((bf16[16,96,128]{2,1,0:T(8,128)(2,1)}), bf16[16,96,128]{2,1,0:T(8,128)(2,1)S(1)}, u32[]{:S(2)}, u32[]{:S(2)}) %all-to-all-start.4) | async-done | bytes 393248 | tf_op jit(solution)/shard_map/all_to_all | solution.py:48
  (91 shorter events, 26.2 us)
Async XLA Ops:
  0.6 16.6 %copy-start = (bf16[1024,128]{1,0:T(8,128)(2,1)S(1)}, bf16[1024,128]{1,0:T(8,128)(2,1)}, u32[]{:S(2)}) copy-start(bf16[1024,128]{1,0:T(8,128)(2,1)} %param.12) | copy-start | bytes 786436
  0.6 16.2 %copy-start.6 = (bf16[64,32]{0,1:T(8,128)(2,1)S(1)}, bf16[64,32]{0,1:T(8,128)(2,1)}, u32[]{:S(2)}) copy-start(bf16[64,32]{0,1:T(8,128)(2,1)} %param.10) | copy-start | bytes 12292
  0.7 16.6 %copy-start.5 = (bf16[16,32,128]{2,1,0:T(8,128)(2,1)S(1)}, bf16[16,32,128]{2,1,0:T(8,128)(2,1)}, u32[]{:S(2)}) copy-start(bf16[16,32,128]{2,1,0:T(8,128)(2,1)} %param.13) | copy-start | bytes 393220
  3.2 2.1 %copy-start.4 = (f32[64,16]{1,0:T(8,128)}, f32[64,16]{1,0:T(8,128)S(1)}, u32[]{:S(2)}) copy-start(f32[64,16]{1,0:T(8,128)S(1)} %add_rsqrt_fusion) | copy-start | bytes 12292
  7.3 28.9 %collective-permute-start = (bf16[64,512]{1,0:T(8,128)(2,1)}, bf16[64,512]{1,0:T(8,128)(2,1)}, u32[]{:S(2)}, u32[]{:S(2)}) collective-permute-start(bf16[64,512]{1,0:T(8,128)(2,1)} %reshape_reshape.9), channel_id=1, source_target_pairs={{0,16},{1,48},{2,80},{3,112},{4,144},{5,176},{6,208},{7,240},{8,27... | collective-permute-start | bytes 196616 | tf_op jit(solution)/shard_map/ppermute | solution.py:36
  14.9 21.3 %collective-permute-start.1 = (bf16[64,512]{1,0:T(8,128)(2,1)}, bf16[64,512]{1,0:T(8,128)(2,1)}, u32[]{:S(2)}, u32[]{:S(2)}) collective-permute-start(bf16[64,512]{1,0:T(8,128)(2,1)} %reshape_reshape.9), channel_id=1, source_target_pairs={{0,0},{1,32},{2,64},{3,96},{4,128},{5,160},{6,192},{7,224},{8,256}... | collective-permute-start | bytes 196616 | tf_op jit(solution)/shard_map/ppermute | solution.py:36
  49.8 3.7 %copy-start.1 = (bf16[256,1024]{1,0:T(8,128)(2,1)S(1)}, bf16[256,1024]{1,0:T(8,128)(2,1)}, u32[]{:S(2)}) copy-start(bf16[256,1024]{1,0:T(8,128)(2,1)} %reshape.167) | copy-start | bytes 1572868
  49.8 4.1 %copy-start.2 = (bf16[256,1024]{1,0:T(8,128)(2,1)S(1)}, bf16[256,1024]{1,0:T(8,128)(2,1)}, u32[]{:S(2)}) copy-start(bf16[256,1024]{1,0:T(8,128)(2,1)} %reshape.162) | copy-start | bytes 1572868
  49.8 5.0 %copy-start.3 = (f32[1024,128]{1,0:T(8,128)S(1)}, f32[1024,128]{1,0:T(8,128)}, u32[]{:S(2)}) copy-start(f32[1024,128]{1,0:T(8,128)} %fusion.19) | copy-start | bytes 1572868
  55.9 62.9 %copy-start.7 = (bf16[64,32]{0,1:T(8,128)(2,1)S(1)}, bf16[64,32]{0,1:T(8,128)(2,1)}, u32[]{:S(2)}) copy-start(bf16[64,32]{0,1:T(8,128)(2,1)} %param.11) | copy-start | bytes 12292
  55.9 62.9 %copy-start.8 = (f32[64]{0:T(128)S(1)}, f32[64]{0:T(128)}, u32[]{:S(2)}) copy-start(f32[64]{0:T(128)} %param.8) | copy-start | bytes 772
  55.9 24.3 %all-to-all-start = ((bf16[16,80,128]{2,1,0:T(8,128)(2,1)}), bf16[16,80,128]{2,1,0:T(8,128)(2,1)S(1)}, u32[]{:S(2)}, u32[]{:S(2)}) async-start(bf16[16,80,128]{2,1,0:T(8,128)(2,1)} %pad_maximum_fusion), calls=%async_computation | async-start | bytes 655360 | tf_op jit(solution)/shard_map/all_to_all | solution.py:48
  80.2 32.3 %all-to-all-start.1 = ((bf16[32,16,128]{2,1,0:T(8,128)(2,1)}), bf16[32,16,128]{2,1,0:T(8,128)(2,1)S(1)}, u32[]{:S(2)}, u32[]{:S(2)}) async-start(bf16[32,16,128]{2,1,0:T(8,128)(2,1)} %reshape.178), calls=%async_computation.1 | async-start | bytes 262144 | tf_op jit(solution)/shard_map/all_to_all | solution.py:48
  112.5 6.2 %collective-permute-start.2 = (f32[16,128]{1,0:T(8,128)S(1)}, f32[16,128]{1,0:T(8,128)S(1)}, u32[]{:S(2)}, u32[]{:S(2)}) collective-permute-start(f32[16,128]{1,0:T(8,128)S(1)} %convert_reduce_fusion.2), channel_id=1, source_target_pairs={{0,0},{1,32},{2,64},{3,96},{4,128},{5,160},{6,192},{7,224},{8,256}... | collective-permute-start | bytes 24584 | tf_op jit(solution)/shard_map/ppermute | solution.py:215
  120.1 29.9 %all-to-all-start.2 = ((f32[32,3,128]{2,1,0:T(4,128)}), f32[32,3,128]{2,1,0:T(4,128)S(1)}, u32[]{:S(2)}, u32[]{:S(2)}) async-start(f32[32,3,128]{2,1,0:T(4,128)} %pad_maximum_fusion.3), calls=%async_computation.2 | async-start | bytes 131072 | tf_op jit(solution)/shard_map/all_to_all | solution.py:48
  150.7 17.9 %all-to-all-start.3 = ((bf16[32,3,128]{2,1,0:T(4,128)(2,1)}), bf16[32,3,128]{2,1,0:T(4,128)(2,1)S(1)}, u32[]{:S(2)}, u32[]{:S(2)}) async-start(bf16[32,3,128]{2,1,0:T(4,128)(2,1)} %broadcast_in_dim.4), calls=%async_computation.3 | async-start | bytes 65536 | tf_op jit(solution)/shard_map/all_to_all | solution.py:48
  169.5 16.8 %all-to-all-start.4 = ((bf16[16,96,128]{2,1,0:T(8,128)(2,1)}), bf16[16,96,128]{2,1,0:T(8,128)(2,1)S(1)}, u32[]{:S(2)}, u32[]{:S(2)}) async-start(bf16[16,96,128]{2,1,0:T(8,128)(2,1)} %broadcast_in_dim.5), calls=%async_computation.4 | async-start | bytes 786432 | tf_op jit(solution)/shard_map/all_to_all | solution.py:48

commit v2 on v1

v2 whole, which is shorter than its diff:
```python
import functools

import jax
import jax.numpy as jnp
from jax import lax
from jax.experimental import pallas as pl
from jax.experimental.pallas import tpu as pltpu
from jax.sharding import PartitionSpec as P

highest = lax.Precision.HIGHEST
LANES = 128
SUBLANES = 8


def swap_pairs(rows, cols, turn):
    ratio = rows // cols
    return [
        (
            source * cols + copy,
            (ratio * copy + (source + turn) % ratio) * cols + source // ratio,
        )
        for source in range(rows)
        for copy in range(cols)
    ]


def home_pairs(rows, cols):
    ratio = rows // cols
    return [
        ((half * cols + share) * cols + col, (ratio * col + half) * cols + share)
        for half in range(ratio)
        for share in range(cols)
        for col in range(cols)
    ]


def trade(pieces, axis):
    return lax.all_to_all(pieces, axis, 0, 0, tiled=True)


def spread(piece, axis):
    extent = lax.axis_size(axis)
    return trade(jnp.broadcast_to(piece[None], (extent,) + piece.shape), axis)


def factor_kernel(
    values_ref,
    stretch_ref,
    offset_ref,
    left_map_ref,
    right_map_ref,
    left_ref,
    right_ref,
    normed_own_ref,
    scaled_own_ref,
    inverse_own_ref,
    normed_ref,
    *,
    shares,
):
    homologs, tokens, width = values_ref.shape
    hidden = left_map_ref.shape[1]
    seq_share = homologs // shares
    values = values_ref[...].astype(jnp.float32)
    mean_value = jnp.mean(values, -1, keepdims=True)
    centred = values - mean_value
    variance = jnp.mean(centred * centred, -1, keepdims=True)
    inverse = lax.rsqrt(variance + 1e-05)
    scaled = centred * inverse
    normed = scaled * stretch_ref[...][None] + offset_ref[...][None]
    normed = normed.astype(jnp.bfloat16).astype(jnp.float32)
    normed_ref[...] = normed.reshape(homologs * tokens, width)

    own = pl.ds(lax.axis_index("col") * seq_share, seq_share)
    own_values = values_ref[own].astype(jnp.float32)
    own_centred = own_values - jnp.mean(own_values, -1, keepdims=True)
    own_inverse = lax.rsqrt(jnp.mean(own_centred * own_centred, -1, keepdims=True) + 1e-05)
    own_scaled = own_centred * own_inverse
    scaled_own_ref[...] = own_scaled
    inverse_own_ref[...] = jnp.broadcast_to(own_inverse, own_scaled.shape)
    normed_own_ref[...] = (own_scaled * stretch_ref[...][None] + offset_ref[...][None]).astype(
        jnp.bfloat16
    )

    maps = jnp.concatenate(
        [left_map_ref[...].astype(jnp.float32).T, right_map_ref[...].astype(jnp.float32).T], 0
    ).astype(jnp.bfloat16)
    for pair in range(tokens // 2):
        block = jnp.concatenate(
            [
                normed_ref[pl.ds((s4 * tokens) + t1 * (tokens // 2) + pair, shares, stride=seq_share * tokens), :]
                for t1 in range(2)
                for s4 in range(seq_share)
            ],
            0,
        ).astype(jnp.bfloat16)
        both = lax.dot_general(
            maps, block, (((1,), (1,)), ((), ())), preferred_element_type=jnp.float32
        ).astype(jnp.bfloat16)
        quad, place = pair // 2, pair % 2
        left_ref[quad * hidden : (quad + 1) * hidden, place * LANES : (place + 1) * LANES] = both[
            :hidden
        ]
        right_ref[pair * hidden : (pair + 1) * hidden, :] = both[hidden:]


def quad_tokens(quad, tokens):
    return [t1 * (tokens // 2) + 2 * quad + place for place in range(2) for t1 in range(2)]


def grad_kernel(
    left_ref, matrix_ref, cotangent_ref, outer_grad_ref, right_out_ref, wide_ref, sum_ref, *, shares
):
    tokens, columns, width = cotangent_ref.shape
    quads = tokens // 4
    hidden = left_ref.shape[0] // quads
    homologs = left_ref.shape[1] // 4
    wide_ref[...] = matrix_ref[...].astype(jnp.float32)
    by_right = jnp.concatenate(
        [wide_ref[pl.ds(e, hidden, stride=hidden), :] for e in range(hidden)], 0
    ).astype(jnp.bfloat16)
    for quad in range(quads):
        block = jnp.concatenate([cotangent_ref[t] for t in quad_tokens(quad, tokens)], 0)
        product = lax.dot_general(
            by_right, block, (((1,), (1,)), ((), ())), preferred_element_type=jnp.float32
        ).astype(jnp.bfloat16)
        for e in range(hidden):
            outer_grad_ref[
                quad * hidden : (quad + 1) * hidden, e * LANES : (e + 1) * LANES
            ] = product[e * hidden : (e + 1) * hidden]

    turned = left_ref[...].astype(jnp.float32).T.astype(jnp.bfloat16)
    lane = lax.broadcasted_iota(jnp.int32, (homologs, LANES), 1)
    quarter = lane // columns
    even = (lane // (columns // 2)) % 2 == 0
    for group in range(hidden // 8):
        product = jnp.dot(
            turned,
            outer_grad_ref[:, group * 8 * LANES : (group + 1) * 8 * LANES],
            preferred_element_type=jnp.float32,
        )
        packed = [None, None]
        for e in range(8):
            part = product[:homologs, e * LANES : (e + 1) * LANES]
            for place in range(1, 4):
                part = jnp.where(
                    quarter == place,
                    product[place * homologs : (place + 1) * homologs, e * LANES : (e + 1) * LANES],
                    part,
                )
            part = part + pltpu.roll(part, LANES // 2, 1)
            part = part + pltpu.roll(part, LANES // 4, 1)
            which, place = e % 2, e // 2
            packed[which] = (
                part if place == 0 else jnp.where(quarter == place, part, packed[which])
            )
        first = jnp.where(even, packed[0], pltpu.roll(packed[1], columns // 2, 1))
        second = jnp.where(even, pltpu.roll(packed[0], LANES - columns // 2, 1), packed[1])
        scale = 1.0 / homologs
        sum_ref[0, group * homologs : (group + 1) * homologs, :] = first * scale
        sum_ref[1, group * homologs : (group + 1) * homologs, :] = second * scale
    for half in range(2):
        for share in range(shares):
            right_out_ref[half * shares + share] = sum_ref[
                half, pl.ds(share, right_out_ref.shape[1], stride=shares), :
            ].astype(jnp.bfloat16)


def pair_kernel(
    left_ref,
    first_ref,
    second_ref,
    outer_grad_ref,
    cotangent_ref,
    out_ref,
    half_ref,
    block_ref,
    outer_ref,
    turn_ref,
):
    tokens, columns, width = cotangent_ref.shape
    quads = tokens // 4
    hidden = left_ref.shape[0] // quads
    homologs = left_ref.shape[1] // 4
    scale = 1.0 / homologs
    shares, share_rows = out_ref.shape[0], turn_ref.shape[0] // out_ref.shape[0]
    straight = lax.axis_index("row") % 2 == 0
    first = first_ref[...].astype(jnp.float32)
    second = second_ref[...].astype(jnp.float32)
    half_ref[0] = jnp.where(straight, first, second)
    half_ref[1] = jnp.where(straight, second, first)
    low = lax.broadcasted_iota(jnp.int32, (SUBLANES, LANES), 1) < LANES // 2
    zero = jnp.zeros((SUBLANES, LANES), jnp.float32)
    block_ref[...] = jnp.zeros_like(block_ref)
    for e in range(hidden):
        lows, highs = [], []
        for half in range(2):
            part = half_ref[half, pl.ds(e, SUBLANES, stride=hidden), :]
            turned = pltpu.roll(part, LANES // 2, 1)
            lows += [jnp.where(low, part, zero), jnp.where(low, turned, zero)]
            highs += [jnp.where(low, zero, turned), jnp.where(low, zero, part)]
        lows = jnp.concatenate(lows, 0).astype(jnp.bfloat16)
        highs = jnp.concatenate(highs, 0).astype(jnp.bfloat16)
        base = e * LANES
        for place in range(4):
            block_ref[
                base + place * columns : base + (place + 1) * columns,
                place // 2 * LANES : (place // 2 + 1) * LANES,
            ] = lows if place % 2 == 0 else highs

    left = left_ref[...]
    for group in range(hidden // 8):
        outer = lax.dot_general(
            left,
            block_ref[group * 8 * LANES : (group + 1) * 8 * LANES, :],
            (((1,), (1,)), ((), ())),
            preferred_element_type=jnp.float32,
        )
        outer = (outer * scale).astype(jnp.bfloat16)
        for step in range(8):
            e = group * 8 + step
            for quad in range(quads):
                outer_ref[
                    e * hidden : (e + 1) * hidden, quad * LANES : (quad + 1) * LANES
                ] = outer[quad * hidden : (quad + 1) * hidden, step * LANES : (step + 1) * LANES]
    cotangent = jnp.concatenate(
        [cotangent_ref[t] for quad in range(quads) for t in quad_tokens(quad, tokens)], 0
    )
    weight_rows = out_ref.shape[1] - share_rows
    for share in range(shares):
        out_ref[share, share_rows:, :] = jnp.dot(
            outer_ref[share * weight_rows : (share + 1) * weight_rows, :],
            cotangent,
            preferred_element_type=jnp.float32,
        ).astype(jnp.bfloat16)
    left_part = jnp.dot(
        outer_grad_ref[...], block_ref[...], preferred_element_type=jnp.float32
    )
    turn_ref[...] = (left_part * scale).T
    for share in range(shares):
        out_ref[share, :share_rows, :] = turn_ref[
            pl.ds(share, share_rows, stride=shares), :
        ].astype(jnp.bfloat16)


def vmem(count):
    return [pl.BlockSpec(memory_space=pltpu.VMEM)] * count


def norm_gradient_pass(
    left_gradient,
    right_gradient,
    lefthand_mapping_tensor,
    righthand_mapping_tensor,
    multiplied_activations,
    reciprocal_spread_std,
    learned_affine_stretch,
):
    hidden = lefthand_mapping_tensor.shape[1]
    both = jnp.concatenate([left_gradient, right_gradient], -1).reshape(-1, 2 * hidden)
    maps = jnp.concatenate([lefthand_mapping_tensor, righthand_mapping_tensor], 1)
    hidden_grad = jnp.dot(both, maps.astype(jnp.float32).T, precision=highest)
    hidden_grad = hidden_grad.reshape(multiplied_activations.shape) * learned_affine_stretch
    mean_one = jnp.mean(hidden_grad, -1, keepdims=True)
    mean_two = jnp.mean(hidden_grad * multiplied_activations, -1, keepdims=True)
    return (
        reciprocal_spread_std * (hidden_grad - mean_one - multiplied_activations * mean_two)
    ).astype(jnp.bfloat16)


def weight_grad(standardized_activations, factor_grad):
    feature_width = standardized_activations.shape[-1]
    hidden = factor_grad.shape[-1]
    return lax.dot_general(
        standardized_activations.astype(jnp.float32).reshape(-1, feature_width),
        factor_grad.reshape(-1, hidden),
        (((0,), (0,)), ((), ())),
        precision=highest,
        preferred_element_type=jnp.float32,
    )


def on_device(
    incoming_evolution_embedding,
    learned_affine_stretch,
    learned_affine_offset,
    lefthand_mapping_tensor,
    righthand_mapping_tensor,
    final_outer_matrix,
    residue_couple_cotangent,
):
    homologs, tokens, width = incoming_evolution_embedding.shape
    hidden = lefthand_mapping_tensor.shape[1]
    pair_width = final_outer_matrix.shape[1]
    columns = residue_couple_cotangent.shape[1]
    rows, cols = lax.axis_size("row"), lax.axis_size("col")
    seq_share = homologs // cols
    quads = tokens // 4
    everywhere = ("row", "col")
    bf16, f32 = jnp.bfloat16, jnp.float32
    left, right, normed_own, scaled_own, inverse_own = pl.pallas_call(
        functools.partial(factor_kernel, shares=cols),
        out_shape=[
            jax.ShapeDtypeStruct((quads * hidden, 4 * homologs), bf16),
            jax.ShapeDtypeStruct((tokens // 2 * hidden, 2 * homologs), bf16),
            jax.ShapeDtypeStruct((seq_share, tokens, width), bf16),
            jax.ShapeDtypeStruct((seq_share, tokens, width), f32),
            jax.ShapeDtypeStruct((seq_share, tokens, width), f32),
        ],
        in_specs=vmem(5),
        out_specs=vmem(5),
        scratch_shapes=[pltpu.VMEM((homologs * tokens, width), f32)],
        cost_estimate=pl.CostEstimate(flops=10_000_000, bytes_accessed=400_000, transcendentals=0),
        name="factors",
    )(
        incoming_evolution_embedding,
        learned_affine_stretch.reshape(1, width),
        learned_affine_offset.reshape(1, width),
        lefthand_mapping_tensor,
        righthand_mapping_tensor,
    )
    first = lax.ppermute(right, everywhere, swap_pairs(rows, cols, 0))
    second = lax.ppermute(right, everywhere, swap_pairs(rows, cols, 1))
    home = home_pairs(rows, cols)
    normed_away = lax.ppermute(normed_own, everywhere, [(b, a) for a, b in home])
    outer_grad, right_pieces = pl.pallas_call(
        functools.partial(grad_kernel, shares=cols),
        out_shape=[
            jax.ShapeDtypeStruct((quads * hidden, hidden * LANES), bf16),
            jax.ShapeDtypeStruct((rows, hidden // 8 * seq_share, LANES), bf16),
        ],
        in_specs=vmem(3),
        out_specs=vmem(2),
        scratch_shapes=[
            pltpu.VMEM((hidden * hidden, pair_width), f32),
            pltpu.VMEM((2, hidden // 8 * homologs, LANES), f32),
        ],
        cost_estimate=pl.CostEstimate(
            flops=800_000_000, bytes_accessed=2_000_000, transcendentals=0
        ),
        name="grads",
    )(left, final_outer_matrix, residue_couple_cotangent)
    row_taken = trade(right_pieces, "row")
    share_rows = 4 * seq_share
    weight_share_rows = hidden * hidden // cols
    col_pieces = pl.pallas_call(
        pair_kernel,
        out_shape=jax.ShapeDtypeStruct((cols, share_rows + weight_share_rows, LANES), bf16),
        in_specs=vmem(5),
        out_specs=vmem(1)[0],
        scratch_shapes=[
            pltpu.VMEM((2, tokens // 2 * hidden, 2 * homologs), f32),
            pltpu.VMEM((hidden * LANES, 4 * homologs), bf16),
            pltpu.VMEM((hidden * hidden, quads * LANES), bf16),
            pltpu.VMEM((4 * homologs, quads * hidden), f32),
        ],
        cost_estimate=pl.CostEstimate(
            flops=1_200_000_000, bytes_accessed=2_000_000, transcendentals=0
        ),
        name="pairs",
    )(left, first, second, outer_grad, residue_couple_cotangent)
    col_taken = trade(col_pieces, "col")

    right_sum = jnp.sum(row_taken.astype(f32), 0)
    right_home = lax.ppermute(right_sum, everywhere, home)

    def right_order(summed):
        summed = summed.reshape(hidden // 8, seq_share, 8, tokens).transpose(1, 3, 0, 2)
        return summed.reshape(seq_share, tokens, hidden)

    right_weight = weight_grad(normed_away, right_order(right_sum))
    col_sum = jnp.sum(col_taken.astype(f32), 0)
    left_gradient = (
        col_sum[:share_rows]
        .reshape(2, 2, seq_share, quads, hidden)
        .transpose(2, 1, 3, 0, 4)
        .reshape(seq_share, tokens, hidden)
    )
    left_weight = weight_grad(normed_own, left_gradient)
    both_weight = jnp.concatenate([left_weight, right_weight], 1).reshape(rows, -1, pair_width)
    weight_rows = weight_share_rows // rows
    row_pieces = jnp.concatenate(
        [col_sum[share_rows:].reshape(rows, weight_rows, pair_width), both_weight], 1
    )
    row_sum = jnp.sum(trade(row_pieces.astype(bf16), "row").astype(f32), 0)
    gathered = spread(row_sum.astype(bf16), "row")
    weight_full = gathered[:, :weight_rows].reshape(-1, pair_width)
    both_part = gathered[:, weight_rows:].reshape(-1, pair_width)
    last = spread(jnp.concatenate([weight_full, both_part], 0), "col").astype(f32)
    inverse_tokens = 1.0 / (tokens * rows)
    output_weight = (
        (last[:, :weight_share_rows] * inverse_tokens)
        .reshape(hidden, hidden, pair_width)
        .transpose(1, 0, 2)
        .reshape(hidden * hidden, pair_width)
    )
    both_total = jnp.sum(last[:, weight_share_rows:], 0) * inverse_tokens
    both_total = both_total.reshape(width, 2 * hidden)
    alignment_gradient = norm_gradient_pass(
        left_gradient,
        right_order(right_home),
        lefthand_mapping_tensor,
        righthand_mapping_tensor,
        scaled_own,
        inverse_own,
        learned_affine_stretch,
    )
    return (alignment_gradient, both_total[:, :hidden], both_total[:, hidden:], output_weight)


def solution(mesh):
    in_specs = (P(None, "row", None), P(), P(), P(), P(), P(), P("row", "col", None))
    out_specs = (P("col", "row", None), P(), P(), P())
    return jax.shard_map(
        on_device, mesh=mesh, in_specs=in_specs, out_specs=out_specs, check_vma=False
    )
```

time: 190 us -> 158 us (0.83)
  blocking collectives: 0 us -> 35 us
  local copies, waits for them, and re-layouts: 38.4 us -> 8.07 us
  starting transfers between devices: 73.1 us -> 51.4 us
  Pallas kernels: 0 us -> 9.88 us
  other arithmetic: 11 us -> 1.65 us
  waiting for transfers between devices: 59 us -> 49.7 us
  matrix products: 6.14 us -> 0.65 us
    all_to_all x0 -> x1, blocking collectives: none -> 35 us  [trade(): return lax.all_to_all(pieces, axis, 0, 0, tiled=True)]
    reshape x18 -> x4, local copies, waits for them, and re-layouts: 32.9 us -> 0.32 us  [the longest x2 0.15 us: right_order(): summed.reshape(hidden // 8, seq_share, 8, tokens).transpose(1, 3, 0, 2)]
    all_to_all x5 -> x4, starting transfers between devices: 59.1 us -> 33 us  [trade(): return lax.all_to_all(pieces, axis, 0, 0, tiled=True)]
    all_to_all x5 -> x4, waiting for transfers between devices: 57.5 us -> 47.1 us  [trade(): return lax.all_to_all(pieces, axis, 0, 0, tiled=True)]
    pallas_call x0 -> x3, Pallas kernels: none -> 9.88 us  [the longest x1 4.18 us: on_device(): pl.pallas_call(pair_kernel, out_shape=jax.ShapeDtypeStruct((cols, share_r...]
    dot_general x14 -> x1, matrix products: 5.89 us -> 0.33 us  [norm_gradient_pass(): hidden_grad = jnp.dot(both, maps.astype(jnp.float32).T, precision=highest)]
    ppermute x3 -> x4, starting transfers between devices: 14 us -> 18.4 us  [the longest x1 6.27 us: on_device(): first = lax.ppermute(right, everywhere, swap_pairs(rows, cols, 0))]
    reduce_sum x7 -> x4, other arithmetic: 3.52 us -> 0.15 us  [the longest x1 0.05 us: on_device(): col_sum = jnp.sum(col_taken.astype(f32), 0)]
  transfers between devices with their start and end apart: 8 -> 8, of which waited for: 6 -> 5; matrix products, arithmetic and copies ran while one was open for 13% -> 2% of each run, Pallas kernels for 0% -> 2%
where the time goes in v2:
time: 158 us; the launch traced here: 157 us
  starting transfers between devices  51.4 us (33%)
  waiting for transfers between devices  49.7 us (31%)
  blocking collectives  35 us (22%)
  Pallas kernels  9.88 us (6%)
  local copies, waits for them, and re-layouts  8.07 us (5%)
  other arithmetic  1.65 us (1%)
    all_to_all x4, waiting for transfers between devices, trade(): return lax.all_to_all(pieces, axis, 0, 0, tiled=True)  47.1 us
    all_to_all x1, blocking collectives, trade(): return lax.all_to_all(pieces, axis, 0, 0, tiled=True)  35 us
    all_to_all x4, starting transfers between devices, trade(): return lax.all_to_all(pieces, axis, 0, 0, tiled=True)  33 us
    ppermute x1, starting transfers between devices, on_device(): first = lax.ppermute(right, everywhere, swap_pairs(rows, cols, 0))  6.27 us
    ppermute x1, starting transfers between devices, on_device(): right_home = lax.ppermute(right_sum, everywhere, home)  4.92 us
    unnamed x23, local copies, waits for them, and re-layouts  4.72 us
    pallas_call x1, Pallas kernels, on_device(): pl.pallas_call(pair_kernel, out_shape=jax.ShapeDtypeStruct((cols, share_r...  4.18 us
    ppermute x1, starting transfers between devices, on_device(): lax.ppermute(normed_own, everywhere, [(b, a) for a, b in home])  3.99 us
  transfers between devices with their start and end apart: 8, of which 5 were waited for; matrix products, arithmetic and copies ran while one was open for 2% of the time, Pallas kernels for 2%

profile of v2, /device:TPU:1, one launch (start us, length us, event | category | flops | bytes accessed | tf_op | source)
XLA Modules:
  0.0 157.3 jit_solution(5690125281640354568)
XLA Ops:
  0.6 1.4 copy.41.left_map_ref
  2.0 0.7 copy.42.right_map_ref
  2.7 2.4 %factors.1 = (bf16[128,256]{1,0:T(8,128)(2,1)}, bf16[256,128]{1,0:T(8,128)(2,1)}, bf16[4,16,64]{2,1,0:T(8,128)(2,1)}, f32[4,16,64]{2,1,0:T(8,128)}, f32[4,16,64]{2,1,0:T(8,128)}) custom-call(bf16[64,16,64]{2,1,0:T(8,128)(2,1)} %values_ref.1, f32[1,64]{1,0:T(1,128)} %bitcast.43, f32[1,64]{1,0:T(1,128)} %bitcast.44, bf16[64,32]{1,0:T(8,128)(2,1)} %copy.41.left_map_ref, ...), custom_call_target="tpu_custom_call" | custom-call | flops 10000000 | bytes 400000 | tf_op jit(solution)/shard_map/factors/pallas_call | solution.py:301
  5.2 6.3 %collective-permute-start = (bf16[256,128]{1,0:T(8,128)(2,1)}, bf16[256,128]{1,0:T(8,128)(2,1)S(1)}, u32[]{:S(2)}, u32[]{:S(2)}) collective-permute-start(bf16[256,128]{1,0:T(8,128)(2,1)} %get-tuple-element.13), channel_id=1, source_target_pairs={{0,0},{1,32},{2,64},{3,96},{4,128},{5,160},{6,192},{7,224},{8,256}... | collective-permute-start | bytes 196616 | tf_op jit(solution)/shard_map/ppermute | solution.py:322
  11.4 3.3 %collective-permute-start.1 = (bf16[256,128]{1,0:T(8,128)(2,1)}, bf16[256,128]{1,0:T(8,128)(2,1)S(1)}, u32[]{:S(2)}, u32[]{:S(2)}) collective-permute-start(bf16[256,128]{1,0:T(8,128)(2,1)} %get-tuple-element.13), channel_id=1, source_target_pairs={{0,16},{1,48},{2,80},{3,112},{4,144},{5,176},{6,208},{7,240},{8,27... | collective-permute-start | bytes 196616 | tf_op jit(solution)/shard_map/ppermute | solution.py:323
  14.7 3.3 %grads.1 = (bf16[128,4096]{1,0:T(8,128)(2,1)}, bf16[32,16,128]{2,1,0:T(8,128)(2,1)}) custom-call(bf16[128,256]{1,0:T(8,128)(2,1)} %get-tuple-element.12.left_ref, bf16[1024,128]{1,0:T(8,128)(2,1)} %matrix_ref.1, bf16[16,32,128]{2,1,0:T(8,128)(2,1)} %cotangent_ref.3), custom_call_target="tpu_custom_call" | custom-call | flops 800000000 | bytes 2000000 | tf_op jit(solution)/shard_map/grads/pallas_call | solution.py:326
  18.0 2.6 %collective-permute-done.1.second_ref = bf16[256,128]{1,0:T(8,128)(2,1)S(1)} collective-permute-done((bf16[256,128]{1,0:T(8,128)(2,1)}, bf16[256,128]{1,0:T(8,128)(2,1)S(1)}, u32[]{:S(2)}, u32[]{:S(2)}) %collective-permute-start.1) | collective-permute-done | bytes 65568 | tf_op jit(solution)/shard_map/ppermute | solution.py:323
  21.2 4.2 %pairs.1 = bf16[16,80,128]{2,1,0:T(8,128)(2,1)} custom-call(bf16[128,256]{1,0:T(8,128)(2,1)} %get-tuple-element.12.left_ref, bf16[256,128]{1,0:T(8,128)(2,1)} %copy-done.6, bf16[256,128]{1,0:T(8,128)(2,1)} %copy-done.7, bf16[128,4096]{1,0:T(8,128)(2,1)} %get-tuple-element.14.outer_grad_ref, bf16[16,32,128]{2,1,0:T(8,128)(2,1)} %cotangent_ref.3), custom_call_target="tpu_custom_call" | custom-call | flops 1200000000 | bytes 2000000 | tf_op jit(solution)/shard_map/pairs/pallas_call | solution.py:346
  25.4 35.0 %all_to_all.25 = bf16[16,80,128]{2,1,0:T(8,128)(2,1)S(1)} all-to-all(bf16[16,80,128]{2,1,0:T(8,128)(2,1)} %pairs.1), channel_id=1, replica_groups=mesh['row'=32,'col'=16] {'col'}, dimensions={0} | all-to-all | bytes 655360 | tf_op jit(solution)/shard_map/all_to_all | solution.py:38
  60.5 9.1 %all-to-all-start.1 = ((bf16[32,16,128]{2,1,0:T(8,128)(2,1)}), bf16[32,16,128]{2,1,0:T(8,128)(2,1)S(1)}, u32[]{:S(2)}, u32[]{:S(2)}) async-start(bf16[32,16,128]{2,1,0:T(8,128)(2,1)} %get-tuple-element.15), calls=%async_computation.1 | async-start | bytes 262144 | tf_op jit(solution)/shard_map/all_to_all | solution.py:38
  69.6 4.0 %collective-permute-start.3 = (bf16[4,16,64]{2,1,0:T(8,128)(2,1)S(1)}, bf16[4,16,64]{2,1,0:T(8,128)(2,1)S(1)}, u32[]{:S(2)}, u32[]{:S(2)}) collective-permute-start(bf16[4,16,64]{2,1,0:T(8,128)(2,1)S(1)} %copy-done.8), channel_id=1, source_target_pairs={{0,0},{32,1},{64,2},{96,3},{128,4},{160,5},{192,6},{224,7},{256,8}... | collective-permute-start | bytes 24584 | tf_op jit(solution)/shard_map/ppermute | solution.py:325
  74.0 12.2 %all-to-all-done.1 = bf16[32,16,128]{2,1,0:T(8,128)(2,1)S(1)} async-done(((bf16[32,16,128]{2,1,0:T(8,128)(2,1)}), bf16[32,16,128]{2,1,0:T(8,128)(2,1)S(1)}, u32[]{:S(2)}, u32[]{:S(2)}) %all-to-all-start.1) | async-done | bytes 131104 | tf_op jit(solution)/shard_map/all_to_all | solution.py:38
  86.2 4.9 %collective-permute-start.2 = (f32[16,128]{1,0:T(8,128)S(1)}, f32[16,128]{1,0:T(8,128)S(1)}, u32[]{:S(2)}, u32[]{:S(2)}) collective-permute-start(f32[16,128]{1,0:T(8,128)S(1)} %convert_reduce_fusion.1), channel_id=1, source_target_pairs={{0,0},{1,32},{2,64},{3,96},{4,128},{5,160},{6,192},{7,224},{8,256}... | collective-permute-start | bytes 24584 | tf_op jit(solution)/shard_map/ppermute | solution.py:365
  92.3 12.8 %all-to-all-start.2 = ((bf16[32,3,128]{2,1,0:T(4,128)(2,1)}), bf16[32,3,128]{2,1,0:T(4,128)(2,1)S(1)}, u32[]{:S(2)}, u32[]{:S(2)}) async-start(bf16[32,3,128]{2,1,0:T(4,128)(2,1)} %pad_maximum_fusion), calls=%async_computation.2 | async-start | bytes 65536 | tf_op jit(solution)/shard_map/all_to_all | solution.py:38
  105.3 13.9 %all-to-all-done.2 = bf16[32,3,128]{2,1,0:T(4,128)(2,1)S(1)} async-done(((bf16[32,3,128]{2,1,0:T(4,128)(2,1)}), bf16[32,3,128]{2,1,0:T(4,128)(2,1)S(1)}, u32[]{:S(2)}, u32[]{:S(2)}) %all-to-all-start.2) | async-done | bytes 24608 | tf_op jit(solution)/shard_map/all_to_all | solution.py:38
  119.8 4.0 %all-to-all-start.3 = ((bf16[32,3,128]{2,1,0:T(4,128)(2,1)}), bf16[32,3,128]{2,1,0:T(4,128)(2,1)S(1)}, u32[]{:S(2)}, u32[]{:S(2)}) async-start(bf16[32,3,128]{2,1,0:T(4,128)(2,1)} %broadcast_in_dim.4), calls=%async_computation.3 | async-start | bytes 65536 | tf_op jit(solution)/shard_map/all_to_all | solution.py:38
  124.8 13.1 %all-to-all-done.3 = bf16[32,3,128]{2,1,0:T(4,128)(2,1)S(1)} async-done(((bf16[32,3,128]{2,1,0:T(4,128)(2,1)}), bf16[32,3,128]{2,1,0:T(4,128)(2,1)S(1)}, u32[]{:S(2)}, u32[]{:S(2)}) %all-to-all-start.3) | async-done | bytes 24608 | tf_op jit(solution)/shard_map/all_to_all | solution.py:38
  138.0 0.8 broadcast_in_dim.5
  138.8 7.1 %all-to-all-start.4 = ((bf16[16,96,128]{2,1,0:T(8,128)(2,1)}), bf16[16,96,128]{2,1,0:T(8,128)(2,1)S(1)}, u32[]{:S(2)}, u32[]{:S(2)}) async-start(bf16[16,96,128]{2,1,0:T(8,128)(2,1)} %broadcast_in_dim.5), calls=%async_computation.4 | async-start | bytes 786432 | tf_op jit(solution)/shard_map/all_to_all | solution.py:38
  145.9 0.7 multiply_convert_fusion
  146.6 7.9 %all-to-all-done.4 = bf16[16,96,128]{2,1,0:T(8,128)(2,1)S(1)} async-done(((bf16[16,96,128]{2,1,0:T(8,128)(2,1)}), bf16[16,96,128]{2,1,0:T(8,128)(2,1)S(1)}, u32[]{:S(2)}, u32[]{:S(2)}) %all-to-all-start.4) | async-done | bytes 393248 | tf_op jit(solution)/shard_map/all_to_all | solution.py:38
  154.9 0.7 copy.54
  155.5 0.7 copy.55
  156.2 1.1 copy.53
  (53 shorter events, 4.3 us)
Async XLA Ops:
  0.6 1.4 copy-start.4
  5.2 12.8 %collective-permute-start = (bf16[256,128]{1,0:T(8,128)(2,1)}, bf16[256,128]{1,0:T(8,128)(2,1)S(1)}, u32[]{:S(2)}, u32[]{:S(2)}) collective-permute-start(bf16[256,128]{1,0:T(8,128)(2,1)} %get-tuple-element.13), channel_id=1, source_target_pairs={{0,0},{1,32},{2,64},{3,96},{4,128},{5,160},{6,192},{7,224},{8,256}... | collective-permute-start | bytes 196616 | tf_op jit(solution)/shard_map/ppermute | solution.py:322
  11.4 9.2 %collective-permute-start.1 = (bf16[256,128]{1,0:T(8,128)(2,1)}, bf16[256,128]{1,0:T(8,128)(2,1)S(1)}, u32[]{:S(2)}, u32[]{:S(2)}) collective-permute-start(bf16[256,128]{1,0:T(8,128)(2,1)} %get-tuple-element.13), channel_id=1, source_target_pairs={{0,16},{1,48},{2,80},{3,112},{4,144},{5,176},{6,208},{7,240},{8,27... | collective-permute-start | bytes 196616 | tf_op jit(solution)/shard_map/ppermute | solution.py:323
  18.0 2.6 %copy-start.6 = (bf16[256,128]{1,0:T(8,128)(2,1)}, bf16[256,128]{1,0:T(8,128)(2,1)S(1)}, u32[]{:S(2)}) copy-start(bf16[256,128]{1,0:T(8,128)(2,1)S(1)} %collective-permute-done.first_ref) | copy-start | bytes 196612
  20.6 0.6 copy-start.7
  60.5 9.1 %copy-start.8 = (bf16[4,16,64]{2,1,0:T(8,128)(2,1)S(1)}, bf16[4,16,64]{2,1,0:T(8,128)(2,1)}, u32[]{:S(2)}) copy-start(bf16[4,16,64]{2,1,0:T(8,128)(2,1)} %get-tuple-element.17) | copy-start | bytes 24580
  60.5 25.7 %all-to-all-start.1 = ((bf16[32,16,128]{2,1,0:T(8,128)(2,1)}), bf16[32,16,128]{2,1,0:T(8,128)(2,1)S(1)}, u32[]{:S(2)}, u32[]{:S(2)}) async-start(bf16[32,16,128]{2,1,0:T(8,128)(2,1)} %get-tuple-element.15), calls=%async_computation.1 | async-start | bytes 262144 | tf_op jit(solution)/shard_map/all_to_all | solution.py:38
  69.6 21.8 %collective-permute-start.3 = (bf16[4,16,64]{2,1,0:T(8,128)(2,1)S(1)}, bf16[4,16,64]{2,1,0:T(8,128)(2,1)S(1)}, u32[]{:S(2)}, u32[]{:S(2)}) collective-permute-start(bf16[4,16,64]{2,1,0:T(8,128)(2,1)S(1)} %copy-done.8), channel_id=1, source_target_pairs={{0,0},{32,1},{64,2},{96,3},{128,4},{160,5},{192,6},{224,7},{256,8}... | collective-permute-start | bytes 24584 | tf_op jit(solution)/shard_map/ppermute | solution.py:325
  86.2 18.9 %collective-permute-start.2 = (f32[16,128]{1,0:T(8,128)S(1)}, f32[16,128]{1,0:T(8,128)S(1)}, u32[]{:S(2)}, u32[]{:S(2)}) collective-permute-start(f32[16,128]{1,0:T(8,128)S(1)} %convert_reduce_fusion.1), channel_id=1, source_target_pairs={{0,0},{1,32},{2,64},{3,96},{4,128},{5,160},{6,192},{7,224},{8,256}... | collective-permute-start | bytes 24584 | tf_op jit(solution)/shard_map/ppermute | solution.py:365
  92.3 26.8 %all-to-all-start.2 = ((bf16[32,3,128]{2,1,0:T(4,128)(2,1)}), bf16[32,3,128]{2,1,0:T(4,128)(2,1)S(1)}, u32[]{:S(2)}, u32[]{:S(2)}) async-start(bf16[32,3,128]{2,1,0:T(4,128)(2,1)} %pad_maximum_fusion), calls=%async_computation.2 | async-start | bytes 65536 | tf_op jit(solution)/shard_map/all_to_all | solution.py:38
  119.8 4.0 %copy-start = (bf16[64,32]{1,0:T(8,128)(2,1)S(1)}, bf16[64,32]{1,0:T(8,128)(2,1)}, u32[]{:S(2)}) copy-start(bf16[64,32]{1,0:T(8,128)(2,1)} %copy.41.left_map_ref) | copy-start | bytes 12292
  119.8 4.0 %copy-start.1 = (bf16[64,32]{1,0:T(8,128)(2,1)S(1)}, bf16[64,32]{1,0:T(8,128)(2,1)}, u32[]{:S(2)}) copy-start(bf16[64,32]{1,0:T(8,128)(2,1)} %copy.42.right_map_ref) | copy-start | bytes 12292
  119.8 4.0 %copy-start.2 = (f32[4,16,64]{2,1,0:T(8,128)S(1)}, f32[4,16,64]{2,1,0:T(8,128)}, u32[]{:S(2)}) copy-start(f32[4,16,64]{2,1,0:T(8,128)} %get-tuple-element.16) | copy-start | bytes 49156
  119.8 18.0 %all-to-all-start.3 = ((bf16[32,3,128]{2,1,0:T(4,128)(2,1)}), bf16[32,3,128]{2,1,0:T(4,128)(2,1)S(1)}, u32[]{:S(2)}, u32[]{:S(2)}) async-start(bf16[32,3,128]{2,1,0:T(4,128)(2,1)} %broadcast_in_dim.4), calls=%async_computation.3 | async-start | bytes 65536 | tf_op jit(solution)/shard_map/all_to_all | solution.py:38
  123.8 0.7 copy-start.5
  138.8 7.1 %copy-start.3 = (f32[4,16,64]{2,1,0:T(8,128)S(1)}, f32[4,16,64]{2,1,0:T(8,128)}, u32[]{:S(2)}) copy-start(f32[4,16,64]{2,1,0:T(8,128)} %get-tuple-element.11) | copy-start | bytes 49156
  138.8 15.8 %all-to-all-start.4 = ((bf16[16,96,128]{2,1,0:T(8,128)(2,1)}), bf16[16,96,128]{2,1,0:T(8,128)(2,1)S(1)}, u32[]{:S(2)}, u32[]{:S(2)}) async-start(bf16[16,96,128]{2,1,0:T(8,128)(2,1)} %broadcast_in_dim.5), calls=%async_computation.4 | async-start | bytes 786432 | tf_op jit(solution)/shard_map/all_to_all | solution.py:38
